TPU v7x, 32 devices: a whole 2x2x4 slice. The times are simulated.
32 devices in a mesh: group: 4 (over x, core), replica: 8 (over z, y).
Axes of the slice: x: 2, y: 2, z: 4, core: 2. Of those that a mesh axis runs over, the one named last changes fastest.
Arguments:
- grad_parts: bfloat16 [8, 8, 128, 512], P('replica', None, 'group'), may hold values from -1 to 1
- owner_order: int32 [8], replicated, may hold values from 0 to 7, each once
- step_count: int32 [1], replicated, may hold values from 1 to 12
- stat_old: float32 [8, 512, 512], P('replica'), as said below
- root_old: bfloat16 [8, 512, 512], P('replica'), may hold values from -0.25 to 0.25
Outputs:
- update: bfloat16 [8, 128, 512], P(None, 'group')
- stat_new: float32 [8, 512, 512], P('replica')
- root_new: bfloat16 [8, 512, 512], P('replica')
Inputs may be any that keep to these rules, and one draw needn't show every extreme that they name: `stat_old`: each matrix is symmetric positive definite.
All inputs are finite; a program needn't handle non-finite values.
Results may differ from a plain program's by a relative error of at most 0.001.
The roundings to bfloat16 on the way count: a program that leaves them out, or rounds other values in their place, can miss the bound.
Values may be sent and summed in bfloat16 or wider, within the bound.
No kernel may reach another device: no remote copies, remote signals or barrier semaphores. Data moves between devices by JAX's collectives and lax.ppermute only.
A program may use at most 64 MiB of HBM per device.

v0:
```python
import jax
import jax.numpy as jnp
from jax import lax
from jax.sharding import PartitionSpec as P

ITERS = 3
decay_rate = 0.95
epsilon = 0.001


def newton(shifted):
    identity = jnp.eye(shifted.shape[0], dtype=jnp.float32)
    frobenius = jnp.sqrt(jnp.sum(shifted * shifted))
    coupled = shifted / frobenius
    root_iter = identity * frobenius ** (-0.25)
    for repeat in range(ITERS):
        factor = (5.0 * identity - coupled) * 0.25
        root_iter = jnp.dot(root_iter, factor, precision=lax.Precision.HIGHEST)
        if repeat + 1 < ITERS:
            factor_sq = jnp.dot(factor, factor, precision=lax.Precision.HIGHEST)
            factor_quad = jnp.dot(factor_sq, factor_sq, precision=lax.Precision.HIGHEST)
            coupled = jnp.dot(factor_quad, coupled, precision=lax.Precision.HIGHEST)
    return root_iter


def local(grad_parts, owner_order, step_count, stat_old, root_old):
    local_grads = grad_parts[0]
    ordered = local_grads[owner_order]
    received = lax.all_to_all(ordered[None], "replica", split_axis=1, concat_axis=0, tiled=True)
    owned = jnp.sum(received.astype(jnp.float32), axis=0)
    partial_gram = jnp.einsum("bri,brj->bij", owned, owned, precision=lax.Precision.HIGHEST)
    products = jnp.einsum(
        "bri,bij->brj", owned.astype(jnp.bfloat16), root_old, preferred_element_type=jnp.float32
    )
    partial_norm = jnp.sum(products * products, axis=(1, 2))
    gram_matrix, update_norm = lax.psum((partial_gram, partial_norm), "group")
    grad_norm = jnp.trace(gram_matrix, axis1=1, axis2=2)
    graft_scale = jnp.sqrt(grad_norm / (update_norm + 1e-06))
    scaled = (graft_scale[:, None, None] * products).astype(jnp.bfloat16)
    gathered = lax.all_gather(scaled, "replica", axis=0, tiled=True)
    update = jnp.zeros_like(gathered).at[owner_order].set(gathered)
    stat_new = decay_rate * stat_old + (1.0 - decay_rate) * gram_matrix
    correction = 1.0 / (1.0 - decay_rate ** step_count[0].astype(jnp.float32))
    shifted = stat_new * correction + epsilon * jnp.eye(stat_new.shape[1], dtype=jnp.float32)
    root_new = lax.map(newton, shifted).astype(jnp.bfloat16)
    return (update, stat_new, root_new)


def solution(mesh):
    placed = (
        P("replica", None, "group", None),
        P(),
        P(),
        P("replica", None, None),
        P("replica", None, None),
    )
    return jax.shard_map(
        local,
        mesh=mesh,
        in_specs=placed,
        out_specs=(P(None, "group", None), P("replica", None, None), P("replica", None, None)),
        check_vma=False,
    )
```

profile of v0, /device:TPU:0, one launch (start us, length us, event | category | flops | bytes accessed | tf_op | source)
XLA Modules:
  0.0 126.4 jit_solution(15580995075982099753)
XLA Ops:
  7.2 0.0 copy-start
  7.2 0.0 all-reduce.2.cloned.1.call-start
  7.2 0.7 compare_select_fusion
  7.9 1.5 %gather_fusion = bf16[8,32,512]{2,1,0:T(8,128)(2,1)S(1)} fusion(bf16[8,32,512]{2,1,0:T(8,128)(2,1)} %bitcast.40, s32[1024]{0:T(1024)S(1)} %pad_clamp_fusion), kind=kCustom, calls=%fused_computation | custom fusion | bytes 524320 | tf_op jit(solution)/shard_map/gather | solution.py:28
  9.5 16.0 %all_to_all.4 = bf16[1,8,32,512]{3,2,0,1:T(8,128)(2,1)S(1)} all-to-all(bf16[1,8,32,512]{3,2,0,1:T(8,128)(2,1)S(1)} %bitcast.38), channel_id=1, replica_groups=mesh['group'=4,'replica'=8] {'replica'}, dimensions={1} | all-to-all | bytes 524288 | tf_op jit(solution)/shard_map/all_to_all | solution.py:29
  25.5 2.0 %convolution_bitcast_fusion = f32[1,512,512]{2,1,0:T(8,128)} fusion(f32[32,512]{1,0:T(8,128)S(1)} %convert_reduce_fusion), kind=kOutput, calls=%fused_computation.5 | convolution fusion | flops 100663296 | bytes 1114112 | tf_op jit(solution)/shard_map/bri,brj->bij/dot_general | solution.py:31
  27.5 0.0 copy-start.1
  27.5 0.0 all-reduce.2.cloned.1.call-update
  28.4 0.0 copy-done
  28.4 0.8 multiply_reduce_fusion.1
  29.2 6.3 %psum.15 = f32[1]{0:T(128)} all-reduce(f32[1]{0:T(128)} %bitcast.5), channel_id=1, replica_groups=mesh['group'=4,'replica'=8] {'group'}, use_global_device_ids=true, to_apply=%region_4.5 | all-reduce | flops 1 | bytes 8 | tf_op jit(solution)/shard_map/psum | solution.py:36
  36.1 26.8 %all-reduce.2.cloned.1.call-done = f32[1,512,512]{2,1,0:T(8,128)} async-done(((f32[1,512,512]{2,1,0:T(8,128)}), f32[1,512,512]{2,1,0:T(8,128)}) %all-reduce.2.cloned.1.call-update) | async-done | bytes 1048592 | tf_op jit(solution)/shard_map/psum | solution.py:36
  63.0 0.0 copy-done.1
  63.0 2.2 %multiply_reduce_fusion = (f32[]{:T(128)}, f32[1,512,512]{2,1,0:T(8,128)S(1)}, f32[]{:T(128)}) fusion(f32[]{:T(128)} %bitcast.8, f32[1,512,512]{2,1,0:T(8,128)} %all-reduce.2.cloned.1.call-done, f32[1,512,512]{2,1,0:T(8,128)S(1)} %copy-done.1), kind=kLoop, calls=%fused_computation.21 | loop fusion | flops 2883582 | bytes 3145740 | tf_op jit(solution)/shard_map/while/body/eval_jaxpr/reduce_sum | solution.py:13
  65.1 0.0 copy-start.2
  65.8 2.1 %fusion.6 = f32[512,512]{1,0:T(8,128)S(1)} fusion(f32[1,512,512]{2,1,0:T(8,128)S(1)} %get-tuple-element.13, f32[]{:T(128)S(6)} %sqrt.8, f32[]{:T(128)} %bitcast.8), kind=kOutput, calls=%fused_computation.12 | convolution fusion | flops 1612709888 | bytes 2097160 | tf_op jit(solution)/shard_map/while/body/eval_jaxpr/dot_general | solution.py:20
  67.9 0.0 copy-done.2
  67.9 1.8 %fusion.51 = f32[512,512]{1,0:T(8,128)S(1)} fusion(f32[512,512]{1,0:T(8,128)S(1)} %fusion.6), kind=kOutput, calls=%fused_computation.63 | convolution fusion | flops 1610612736 | bytes 2097152 | tf_op jit(solution)/shard_map/while/body/eval_jaxpr/dot_general | solution.py:21
  69.8 3.1 %fusion.8 = f32[512,512]{1,0:T(8,128)S(1)} fusion(f32[512,512]{1,0:T(8,128)S(1)} %fusion.51, f32[1,512,512]{2,1,0:T(8,128)} %copy-done.2, f32[]{:T(128)S(6)} %sqrt.8, f32[]{:T(128)} %bitcast.8), kind=kOutput, calls=%fused_computation.14 | convolution fusion | flops 1611923456 | bytes 3145736 | tf_op jit(solution)/shard_map/while/body/eval_jaxpr/dot_general | solution.py:22
  72.9 1.9 %fusion.16 = f32[512,512]{1,0:T(8,128)S(1)} fusion(f32[512,512]{1,0:T(8,128)S(1)} %fusion.8), kind=kOutput, calls=%fused_computation.28 | convolution fusion | flops 1611661312 | bytes 2097152 | tf_op jit(solution)/shard_map/while/body/eval_jaxpr/dot_general | solution.py:20
  74.9 1.8 %fusion.52 = f32[512,512]{1,0:T(8,128)S(1)} fusion(f32[512,512]{1,0:T(8,128)S(1)} %fusion.16), kind=kOutput, calls=%fused_computation.64 | convolution fusion | flops 1610612736 | bytes 2097152 | tf_op jit(solution)/shard_map/while/body/eval_jaxpr/dot_general | solution.py:21
  76.7 1.9 %fusion = f32[512,512]{1,0:T(8,128)S(1)} fusion(f32[512,512]{1,0:T(8,128)S(1)} %fusion.52, f32[512,512]{1,0:T(8,128)S(1)} %fusion.8), kind=kOutput, calls=%fused_computation.6 | convolution fusion | flops 1611661312 | bytes 3145728 | tf_op jit(solution)/shard_map/while/body/eval_jaxpr/dot_general | solution.py:22
  78.6 3.3 %fusion.3 = f32[512,512]{1,0:T(8,128)S(1)} fusion(f32[]{:T(128)S(6)} %pow.9, f32[1,512,512]{2,1,0:T(8,128)} %copy-done.2, f32[]{:T(128)S(6)} %sqrt.8, f32[]{:T(128)} %bitcast.8), kind=kOutput, calls=%fused_computation.10 | convolution fusion | flops 1613496320 | bytes 2097164 | tf_op jit(solution)/shard_map/while/body/eval_jaxpr/dot_general | solution.py:18
  82.0 1.9 %fusion.18 = f32[512,512]{1,0:T(8,128)S(1)} fusion(f32[512,512]{1,0:T(8,128)S(1)} %fusion.3, f32[512,512]{1,0:T(8,128)S(1)} %fusion.8), kind=kOutput, calls=%fused_computation.29 | convolution fusion | flops 1611661312 | bytes 3145728 | tf_op jit(solution)/shard_map/while/body/eval_jaxpr/dot_general | solution.py:18
  84.6 30.8 %all-gather = bf16[256,512]{1,0:T(8,128)(2,1)S(1)} all-gather(bf16[32,512]{1,0:T(8,128)(2,1)S(1)} %multiply_convert_fusion), channel_id=2, replica_groups=mesh['group'=4,'replica'=8] {'replica'}, dimensions={0}, use_global_device_ids=true | all-gather | bytes 294912 | tf_op jit(solution)/shard_map/all_gather | solution.py:40
  115.5 2.6 %fusion.1 = bf16[1,512,512]{2,1,0:T(8,128)(2,1)} fusion(f32[512,512]{1,0:T(8,128)S(1)} %fusion.18, f32[512,512]{1,0:T(8,128)S(1)} %fusion), kind=kOutput, calls=%fused_computation.8 | convolution fusion | flops 1610874880 | bytes 2621440 | tf_op jit(solution)/shard_map/while/body/eval_jaxpr/dot_general | solution.py:18
  118.1 0.8 scatter_fusion
  118.9 0.0 copy-start.3
  118.9 0.7 copy-done.3
  (4 shorter events, 0.1 us)
Async XLA Ops:
  7.2 21.2 %copy-start = (bf16[1,512,512]{2,1,0:T(8,128)(2,1)S(1)}, bf16[1,512,512]{2,1,0:T(8,128)(2,1)}, u32[]{:S(2)}) copy-start(bf16[1,512,512]{2,1,0:T(8,128)(2,1)} %param.9) | copy-start | bytes 1572868
  7.2 55.8 %all-reduce.2.cloned.1.call-start = ((), (), s32[]{:S(2)}) async-start(), calls=%async_computation.1 | async-start | bytes 2097152 | tf_op jit(solution)/shard_map/psum | solution.py:36
  27.5 35.4 %copy-start.1 = (f32[1,512,512]{2,1,0:T(8,128)S(1)}, f32[1,512,512]{2,1,0:T(8,128)}, u32[]{:S(2)}) copy-start(f32[1,512,512]{2,1,0:T(8,128)} %param.8) | copy-start | bytes 3145732
  65.1 2.8 %copy-start.2 = (f32[1,512,512]{2,1,0:T(8,128)}, f32[1,512,512]{2,1,0:T(8,128)S(1)}, u32[]{:S(2)}) copy-start(f32[1,512,512]{2,1,0:T(8,128)S(1)} %get-tuple-element.13) | copy-start | bytes 3145732
  118.9 0.7 copy-start.3
Sparse Core Ops, SparseCore 0:
  27.7 35.2 all-reduce.1
where the time goes:
time: 127 us; the launch traced here: 126 us
  blocking collectives  53.1 us (42%)
  waiting for transfers between devices  26.9 us (21%)
  matrix products  23.4 us (18%)
  between operations  17.1 us (13%)
  local copies, waits for them, and re-layouts  3 us (2%)
  other arithmetic  2.95 us (2%)
    all_gather x1, blocking collectives, local(): gathered = lax.all_gather(scaled, 'replica', axis=0, tiled=True)  30.8 us
    psum x1, waiting for transfers between devices, local(): gram_matrix, update_norm = lax.psum((partial_gram, partial_norm), 'group')  26.8 us
    all_to_all x1, blocking collectives, local(): lax.all_to_all(ordered[None], 'replica', split_axis=1, concat_axis=0, til...  16 us
    dot_general x3, matrix products, newton(): root_iter = jnp.dot(root_iter, factor, precision=lax.Precision.HIGHEST)  7.9 us
    psum x1, blocking collectives, local(): gram_matrix, update_norm = lax.psum((partial_gram, partial_norm), 'group')  6.27 us
    dot_general x2, matrix products, newton(): coupled = jnp.dot(factor_quad, coupled, precision=lax.Precision.HIGHEST)  5 us
    dot_general x2, matrix products, newton(): factor_sq = jnp.dot(factor, factor, precision=lax.Precision.HIGHEST)  3.98 us
    dot_general x2, matrix products, newton(): factor_quad = jnp.dot(factor_sq, factor_sq, precision=lax.Precision.HIGHEST)  3.68 us
  transfers between devices with their start and end apart: 1, of which 1 were waited for; matrix products, arithmetic and copies ran while one was open for 1% of the time, Pallas kernels for 0%

commit v1 on v0

--- a/solution.py
+++ b/solution.py
@@ -6,6 +6,18 @@
 ITERS = 3
 decay_rate = 0.95
 epsilon = 0.001
+
+
+def doubled_up(x, axis, dim):
+    ways, here, step = (lax.axis_size(axis), lax.axis_index(axis), x.shape[dim])
+    line, have = (x, 1)
+    while have < ways:
+        line = jnp.concatenate(
+            [line, lax.ppermute(line, axis, [(d, (d - have) % ways) for d in range(ways)])],
+            axis=dim,
+        )
+        have = 2 * have
+    return jnp.roll(line, here * step, axis=dim)
 
 
 def newton(shifted):
@@ -37,7 +49,7 @@
     grad_norm = jnp.trace(gram_matrix, axis1=1, axis2=2)
     graft_scale = jnp.sqrt(grad_norm / (update_norm + 1e-06))
     scaled = (graft_scale[:, None, None] * products).astype(jnp.bfloat16)
-    gathered = lax.all_gather(scaled, "replica", axis=0, tiled=True)
+    gathered = doubled_up(scaled, "replica", 0)
     update = jnp.zeros_like(gathered).at[owner_order].set(gathered)
     stat_new = decay_rate * stat_old + (1.0 - decay_rate) * gram_matrix
     correction = 1.0 / (1.0 - decay_rate ** step_count[0].astype(jnp.float32))

time: 127 us -> 110 us (0.87)
  blocking collectives: 53.1 us -> 22.3 us
  waiting for transfers between devices: 26.9 us -> 34.5 us
  starting transfers between devices: 0.04 us -> 5.68 us
    all_gather x1 -> x0, blocking collectives: 30.8 us -> none  [local(): gathered = lax.all_gather(scaled, 'replica', axis=0, tiled=True)]
    ppermute x0 -> x3, waiting for transfers between devices: none -> 7.66 us  [doubled_up(): lax.ppermute(line, axis, [(d, (d - have) % ways) for d in range(ways)])]
    ppermute x0 -> x3, starting transfers between devices: none -> 5.64 us  [doubled_up(): lax.ppermute(line, axis, [(d, (d - have) % ways) for d in range(ways)])]
  transfers between devices with their start and end apart: 1 -> 4, of which waited for: 1 -> 3; matrix products, arithmetic and copies ran while one was open for 1% -> 5% of each run, Pallas kernels for 0% -> 0%
where the time goes in v1:
time: 110 us; the launch traced here: 109 us
  waiting for transfers between devices  34.5 us (31%)
  matrix products  23.4 us (21%)
  blocking collectives  22.3 us (20%)
  between operations  17.2 us (16%)
  starting transfers between devices  5.68 us (5%)
  local copies, waits for them, and re-layouts  3.07 us (3%)
  other arithmetic  2.98 us (3%)
    psum x1, waiting for transfers between devices, local(): gram_matrix, update_norm = lax.psum((partial_gram, partial_norm), 'group')  26.8 us
    all_to_all x1, blocking collectives, local(): lax.all_to_all(ordered[None], 'replica', split_axis=1, concat_axis=0, til...  16 us
    dot_general x3, matrix products, newton(): root_iter = jnp.dot(root_iter, factor, precision=lax.Precision.HIGHEST)  7.89 us
    ppermute x3, waiting for transfers between devices, doubled_up(): lax.ppermute(line, axis, [(d, (d - have) % ways) for d in range(ways)])  7.66 us
    psum x1, blocking collectives, local(): gram_matrix, update_norm = lax.psum((partial_gram, partial_norm), 'group')  6.27 us
    ppermute x3, starting transfers between devices, doubled_up(): lax.ppermute(line, axis, [(d, (d - have) % ways) for d in range(ways)])  5.64 us
    dot_general x2, matrix products, newton(): coupled = jnp.dot(factor_quad, coupled, precision=lax.Precision.HIGHEST)  5 us
    dot_general x2, matrix products, newton(): factor_sq = jnp.dot(factor, factor, precision=lax.Precision.HIGHEST)  3.98 us
  transfers between devices with their start and end apart: 4, of which 3 were waited for; matrix products, arithmetic and copies ran while one was open for 5% of the time, Pallas kernels for 0%

profile of v1, /device:TPU:0, one launch (start us, length us, event | category | flops | bytes accessed | tf_op | source)
XLA Modules:
  0.0 109.1 jit_solution(11931011163135831642)
XLA Ops:
  7.2 0.0 copy-start
  7.2 0.0 all-reduce.2.cloned.1.call-start
  7.2 0.7 compare_select_fusion
  7.9 1.5 %gather_fusion = bf16[8,32,512]{2,1,0:T(8,128)(2,1)S(1)} fusion(bf16[8,32,512]{2,1,0:T(8,128)(2,1)} %bitcast.41, s32[1024]{0:T(1024)S(1)} %pad_clamp_fusion), kind=kCustom, calls=%fused_computation | custom fusion | bytes 524320 | tf_op jit(solution)/shard_map/gather | solution.py:40
  9.5 16.0 %all_to_all.4 = bf16[1,8,32,512]{3,2,0,1:T(8,128)(2,1)S(1)} all-to-all(bf16[1,8,32,512]{3,2,0,1:T(8,128)(2,1)S(1)} %bitcast.40), channel_id=1, replica_groups=mesh['group'=4,'replica'=8] {'replica'}, dimensions={1} | all-to-all | bytes 524288 | tf_op jit(solution)/shard_map/all_to_all | solution.py:41
  25.5 2.0 %convolution_bitcast_fusion = f32[1,512,512]{2,1,0:T(8,128)} fusion(f32[32,512]{1,0:T(8,128)S(1)} %convert_reduce_fusion), kind=kOutput, calls=%fused_computation.5 | convolution fusion | flops 100663296 | bytes 1114112 | tf_op jit(solution)/shard_map/bri,brj->bij/dot_general | solution.py:43
  27.5 0.0 copy-start.1
  27.5 0.0 all-reduce.2.cloned.1.call-update
  28.4 0.0 copy-done
  28.4 0.8 multiply_reduce_fusion.1
  29.2 6.3 %psum.15 = f32[1]{0:T(128)} all-reduce(f32[1]{0:T(128)} %bitcast.5), channel_id=1, replica_groups=mesh['group'=4,'replica'=8] {'group'}, use_global_device_ids=true, to_apply=%region_4.5 | all-reduce | flops 1 | bytes 8 | tf_op jit(solution)/shard_map/psum | solution.py:48
  36.1 26.8 %all-reduce.2.cloned.1.call-done = f32[1,512,512]{2,1,0:T(8,128)} async-done(((f32[1,512,512]{2,1,0:T(8,128)}), f32[1,512,512]{2,1,0:T(8,128)}) %all-reduce.2.cloned.1.call-update) | async-done | bytes 1048592 | tf_op jit(solution)/shard_map/psum | solution.py:48
  63.0 0.0 copy-done.1
  63.0 2.2 %multiply_reduce_fusion = (f32[]{:T(128)}, f32[1,512,512]{2,1,0:T(8,128)S(1)}, f32[]{:T(128)}) fusion(f32[]{:T(128)} %bitcast.8, f32[1,512,512]{2,1,0:T(8,128)} %all-reduce.2.cloned.1.call-done, f32[1,512,512]{2,1,0:T(8,128)S(1)} %copy-done.1), kind=kLoop, calls=%fused_computation.21 | loop fusion | flops 2883582 | bytes 3145740 | tf_op jit(solution)/shard_map/while/body/eval_jaxpr/reduce_sum | solution.py:25
  65.1 0.0 copy-start.2
  65.8 2.1 %fusion.6 = f32[512,512]{1,0:T(8,128)S(1)} fusion(f32[1,512,512]{2,1,0:T(8,128)S(1)} %get-tuple-element.13, f32[]{:T(128)S(6)} %sqrt.8, f32[]{:T(128)} %bitcast.8), kind=kOutput, calls=%fused_computation.12 | convolution fusion | flops 1612709888 | bytes 2097160 | tf_op jit(solution)/shard_map/while/body/eval_jaxpr/dot_general | solution.py:32
  67.9 0.0 copy-done.2
  67.9 1.8 %fusion.53 = f32[512,512]{1,0:T(8,128)S(1)} fusion(f32[512,512]{1,0:T(8,128)S(1)} %fusion.6), kind=kOutput, calls=%fused_computation.75 | convolution fusion | flops 1610612736 | bytes 2097152 | tf_op jit(solution)/shard_map/while/body/eval_jaxpr/dot_general | solution.py:33
  69.8 3.1 %fusion.8 = f32[512,512]{1,0:T(8,128)S(1)} fusion(f32[512,512]{1,0:T(8,128)S(1)} %fusion.53, f32[1,512,512]{2,1,0:T(8,128)} %copy-done.2, f32[]{:T(128)S(6)} %sqrt.8, f32[]{:T(128)} %bitcast.8), kind=kOutput, calls=%fused_computation.14 | convolution fusion | flops 1611923456 | bytes 3145736 | tf_op jit(solution)/shard_map/while/body/eval_jaxpr/dot_general | solution.py:34
  72.9 1.9 %fusion.16 = f32[512,512]{1,0:T(8,128)S(1)} fusion(f32[512,512]{1,0:T(8,128)S(1)} %fusion.8), kind=kOutput, calls=%fused_computation.28 | convolution fusion | flops 1611661312 | bytes 2097152 | tf_op jit(solution)/shard_map/while/body/eval_jaxpr/dot_general | solution.py:32
  74.9 1.8 %fusion.54 = f32[512,512]{1,0:T(8,128)S(1)} fusion(f32[512,512]{1,0:T(8,128)S(1)} %fusion.16), kind=kOutput, calls=%fused_computation.76 | convolution fusion | flops 1610612736 | bytes 2097152 | tf_op jit(solution)/shard_map/while/body/eval_jaxpr/dot_general | solution.py:33
  76.7 1.9 %fusion = f32[512,512]{1,0:T(8,128)S(1)} fusion(f32[512,512]{1,0:T(8,128)S(1)} %fusion.54, f32[512,512]{1,0:T(8,128)S(1)} %fusion.8), kind=kOutput, calls=%fused_computation.6 | convolution fusion | flops 1611661312 | bytes 3145728 | tf_op jit(solution)/shard_map/while/body/eval_jaxpr/dot_general | solution.py:34
  78.6 3.3 %fusion.3 = f32[512,512]{1,0:T(8,128)S(1)} fusion(f32[]{:T(128)S(6)} %pow.9, f32[1,512,512]{2,1,0:T(8,128)} %copy-done.2, f32[]{:T(128)S(6)} %sqrt.8, f32[]{:T(128)} %bitcast.8), kind=kOutput, calls=%fused_computation.10 | convolution fusion | flops 1613496320 | bytes 2097164 | tf_op jit(solution)/shard_map/while/body/eval_jaxpr/dot_general | solution.py:30
  82.7 4.3 %collective-permute-start = (bf16[1,32,512]{2,1,0:T(8,128)(2,1)S(1)}, bf16[1,32,512]{2,1,0:T(8,128)(2,1)S(1)}, u32[]{:S(2)}, u32[]{:S(2)}) collective-permute-start(bf16[1,32,512]{2,1,0:T(8,128)(2,1)S(1)} %get-tuple-element.15), channel_id=1, source_target_pairs={{0,7},{1,0},{2,1},{3,2},{4,3},{5,4},{6,5},{7,6},{8,15},{9,8},{10,9... | collective-permute-start | bytes 98312 | tf_op jit(solution)/shard_map/ppermute | solution.py:16
  87.0 1.9 %fusion.18 = f32[512,512]{1,0:T(8,128)S(1)} fusion(f32[512,512]{1,0:T(8,128)S(1)} %fusion.3, f32[512,512]{1,0:T(8,128)S(1)} %fusion.8), kind=kOutput, calls=%fused_computation.29 | convolution fusion | flops 1611661312 | bytes 3145728 | tf_op jit(solution)/shard_map/while/body/eval_jaxpr/dot_general | solution.py:30
  88.9 0.0 collective-permute-done
  89.0 1.1 %collective-permute-start.1 = (bf16[2,32,512]{2,1,0:T(8,128)(2,1)S(1)}, bf16[2,32,512]{2,1,0:T(8,128)(2,1)S(1)}, u32[]{:S(2)}, u32[]{:S(2)}) collective-permute-start(bf16[2,32,512]{2,1,0:T(8,128)(2,1)S(1)} %pad_maximum_fusion.1), channel_id=1, source_target_pairs={{0,6},{1,7},{2,0},{3,1},{4,2},{5,3},{6,4},{7,5},{8,14},{9,15},{10,... | collective-permute-start | bytes 196616 | tf_op jit(solution)/shard_map/ppermute | solution.py:16
  90.1 2.6 %fusion.1 = bf16[1,512,512]{2,1,0:T(8,128)(2,1)} fusion(f32[512,512]{1,0:T(8,128)S(1)} %fusion.18, f32[512,512]{1,0:T(8,128)S(1)} %fusion), kind=kOutput, calls=%fused_computation.8 | convolution fusion | flops 1610874880 | bytes 2621440 | tf_op jit(solution)/shard_map/while/body/eval_jaxpr/dot_general | solution.py:30
  92.7 0.6 collective-permute-done.1
  93.3 0.2 collective-permute-start.2
  93.5 7.1 %collective-permute-done.2 = bf16[4,32,512]{2,1,0:T(8,128)(2,1)S(1)} collective-permute-done((bf16[4,32,512]{2,1,0:T(8,128)(2,1)S(1)}, bf16[4,32,512]{2,1,0:T(8,128)(2,1)S(1)}, u32[]{:S(2)}, u32[]{:S(2)}) %collective-permute-start.2) | collective-permute-done | bytes 131104 | tf_op jit(solution)/shard_map/ppermute | solution.py:16
  100.8 0.8 scatter_fusion
  101.5 0.0 copy-start.3
  101.5 0.7 copy-done.3
  (14 shorter events, 0.2 us)
Async XLA Ops:
  7.2 21.2 %copy-start = (bf16[1,512,512]{2,1,0:T(8,128)(2,1)S(1)}, bf16[1,512,512]{2,1,0:T(8,128)(2,1)}, u32[]{:S(2)}) copy-start(bf16[1,512,512]{2,1,0:T(8,128)(2,1)} %param.9) | copy-start | bytes 1572868
  7.2 55.8 %all-reduce.2.cloned.1.call-start = ((), (), s32[]{:S(2)}) async-start(), calls=%async_computation.1 | async-start | bytes 2097152 | tf_op jit(solution)/shard_map/psum | solution.py:48
  27.5 35.4 %copy-start.1 = (f32[1,512,512]{2,1,0:T(8,128)S(1)}, f32[1,512,512]{2,1,0:T(8,128)}, u32[]{:S(2)}) copy-start(f32[1,512,512]{2,1,0:T(8,128)} %param.8) | copy-start | bytes 3145732
  65.1 2.8 %copy-start.2 = (f32[1,512,512]{2,1,0:T(8,128)}, f32[1,512,512]{2,1,0:T(8,128)S(1)}, u32[]{:S(2)}) copy-start(f32[1,512,512]{2,1,0:T(8,128)S(1)} %get-tuple-element.13) | copy-start | bytes 3145732
  82.7 6.2 %collective-permute-start = (bf16[1,32,512]{2,1,0:T(8,128)(2,1)S(1)}, bf16[1,32,512]{2,1,0:T(8,128)(2,1)S(1)}, u32[]{:S(2)}, u32[]{:S(2)}) collective-permute-start(bf16[1,32,512]{2,1,0:T(8,128)(2,1)S(1)} %get-tuple-element.15), channel_id=1, source_target_pairs={{0,7},{1,0},{2,1},{3,2},{4,3},{5,4},{6,5},{7,6},{8,15},{9,8},{10,9... | collective-permute-start | bytes 98312 | tf_op jit(solution)/shard_map/ppermute | solution.py:16
  89.0 4.3 %collective-permute-start.1 = (bf16[2,32,512]{2,1,0:T(8,128)(2,1)S(1)}, bf16[2,32,512]{2,1,0:T(8,128)(2,1)S(1)}, u32[]{:S(2)}, u32[]{:S(2)}) collective-permute-start(bf16[2,32,512]{2,1,0:T(8,128)(2,1)S(1)} %pad_maximum_fusion.1), channel_id=1, source_target_pairs={{0,6},{1,7},{2,0},{3,1},{4,2},{5,3},{6,4},{7,5},{8,14},{9,15},{10,... | collective-permute-start | bytes 196616 | tf_op jit(solution)/shard_map/ppermute | solution.py:16
  93.3 7.3 %collective-permute-start.2 = (bf16[4,32,512]{2,1,0:T(8,128)(2,1)S(1)}, bf16[4,32,512]{2,1,0:T(8,128)(2,1)S(1)}, u32[]{:S(2)}, u32[]{:S(2)}) collective-permute-start(bf16[4,32,512]{2,1,0:T(8,128)(2,1)S(1)} %pad_maximum_fusion), channel_id=1, source_target_pairs={{0,4},{1,5},{2,6},{3,7},{4,0},{5,1},{6,2},{7,3},{8,12},{9,13},{10,... | collective-permute-start | bytes 393224 | tf_op jit(solution)/shard_map/ppermute | solution.py:16
  101.5 0.7 copy-start.3
Sparse Core Ops, SparseCore 0:
  27.7 35.2 all-reduce.1
